TPU v7x, 128 devices: a whole 4x4x4 slice. The times are simulated.
128 devices in a mesh: gx: 8 (over y, core), gy: 16 (over z, x).
Axes of the slice: x: 4, y: 4, z: 4, core: 2. Of those that a mesh axis runs over, the one named last changes fastest.
Arguments:
- charges: bfloat16 [2048, 256, 64], P(('gx', 'gy')), may hold values from -6 to 6
- leaf_basis: bfloat16 [2048, 256, 64], P(('gx', 'gy')), may hold values from -0.375 to 0.375
- transfer: bfloat16 [128, 24, 64, 64], P(('gx', 'gy')), may hold values from -0.5 to 0.5
- near_blocks: bfloat16 [2048, 6, 256, 256], P(('gx', 'gy')), may hold values from -0.15625 to 0.15625
- near_source: int32 [2048, 6], P(('gx', 'gy')), may hold values from 0 to 2047, as said below
- coupling: bfloat16 [128, 128, 6, 64, 64], P(('gx', 'gy')), may hold values from -0.25 to 0.25
- send_cluster: int32 [128, 128, 6], P(('gx', 'gy')), may hold values from 0 to 27, as said below
- target_cluster: int32 [128, 128, 6], P(('gx', 'gy')), may hold values from 0 to 28, as said below
Outputs:
- potential: bfloat16 [2048, 256, 64], P(('gx', 'gy'))
Inputs may be any that keep to these rules, and one draw needn't show every extreme that they name: `near_source`: leaf l's first source is l itself; the others are distinct offsets o with 0 < |o| <= 8, giving leaf l + o clipped to the range of leaves. send_cluster[p, d, c] is a cluster of device p in the numbering of the steps, on the same level as target_cluster[d, p, c] when that slot is used. target_cluster[d, p, c] is the cluster of device d that receives the slot; the value 28 marks an empty slot. Between devices whose indices differ by at most one all 6 slots are used.
All inputs are finite; a program needn't handle non-finite values.
Results may differ from a plain program's by a relative error of at most 0.0055.
Values may be sent and summed in bfloat16 or wider, within the bound.
No kernel may reach another device: no remote copies, remote signals or barrier semaphores. Data moves between devices by JAX's collectives and lax.ppermute only.
A program may use at most 192 MiB of HBM per device.

v0:
```python
import functools

import jax
import jax.numpy as jnp
from jax import lax
from jax.experimental import pallas as pl
from jax.experimental.pallas import tpu as pltpu
from jax.sharding import PartitionSpec as P

AXES = ("gx", "gy")
LEVELS = 3
GROUP = 4
F32 = jnp.float32
BF16 = jnp.bfloat16


def level_bounds(leaves):
    bounds, offset = [], 0
    for depth in range(LEVELS):
        bounds.append((offset, leaves >> depth))
        offset += leaves >> depth
    return bounds, offset


def contract(a, b, da, db):
    return lax.dot_general(a, b, (((da,), (db,)), ((), ())), preferred_element_type=F32)


def split_pair(x):
    high = x.astype(BF16)
    return high, (x - high.astype(F32)).astype(BF16)


def left_lanes(shape):
    return lax.broadcasted_iota(jnp.int32, shape, 1) < shape[1] // 2


def up_kernel(bounds, slots, send, charges, basis, transfer, out, upward, staged, sems):
    rank = upward.shape[1]
    chunks, rows = staged.shape[:2]
    pairs = slots // 2
    per_chunk = rows // (pairs * rank)

    def put(c, block):
        block = block.astype(BF16)
        upward[c] = jnp.concatenate([block, block], axis=1)
        return block

    held = []
    for leaf in range(bounds[0][1]):
        held.append(put(leaf, contract(basis[leaf], charges[leaf], 1, 1)))
    for depth in range(LEVELS - 1):
        lo, size = bounds[depth]
        above = bounds[depth + 1][0]
        parents = []
        for c in range(size // 2):
            both = jnp.concatenate([transfer[lo + 2 * c], transfer[lo + 2 * c + 1]], axis=0)
            kids = jnp.concatenate([held[2 * c], held[2 * c + 1]], axis=0)
            parents.append(put(above + c, contract(both, kids, 0, 0)))
        held = parents

    def send_out(j):
        rows_out = out.at[pl.ds(pl.multiple_of(j * rows, rows), rows)]
        return pltpu.make_async_copy(staged.at[j], rows_out, sems.at[j])

    left = left_lanes(upward.shape[1:])

    @pl.loop(0, chunks)
    def _(j):
        def copy(i, carry):
            d = j * per_chunk + i
            for q in range(pairs):
                at = pl.multiple_of((i * pairs + q) * rank, rank)
                even, odd = upward[send[2 * q, 0, d]], upward[send[2 * q + 1, 0, d]]
                staged[j, pl.ds(at, rank), :] = jnp.where(left, even, odd)
            return carry

        lax.fori_loop(0, per_chunk, copy, 0, unroll=16)
        send_out(j).start()

    @pl.loop(0, chunks)
    def _(j):
        send_out(j).wait()


def near_kernel(reach, first, source, own, blocks, out, listed, window):
    step = pl.program_id(0)
    leaves = own.shape[0]
    per_step, near = blocks.shape[:2]

    @pl.when(step == 0)
    def _():
        edge = jnp.zeros((reach, *own.shape[1:]), BF16)
        window[pl.ds(0, reach)] = edge
        window[pl.ds(reach, leaves)] = own[...]
        window[pl.ds(reach + leaves, reach)] = edge

        def note(leaf, found):
            for s in range(near):
                row = source[s, leaf] - first[0]
                inside = (row >= 0) & (row < leaves)
                edge_row = jnp.where(row < 0, row + reach, row - leaves + reach)
                listed[found] = edge_row | (s << 8) | (leaf << 16) | (leaf << 24)
                found = found + jnp.where(inside, 0, 1)
            return found

        most = leaves * near + GROUP

        def clear(i, carry):
            listed[i] = leaves << 24
            return carry

        lax.fori_loop(0, most, clear, 0, unroll=GROUP)
        found = lax.fori_loop(0, leaves, note, 0)
        for i in range(GROUP):
            listed[found + i] = leaves << 24
        listed[most] = (found + GROUP - 1) // GROUP

    for i in range(per_step):
        total = None
        for s in range(near):
            row = source[s, step * per_step + i] - first[0] + reach
            term = contract(window[row], blocks[i, s], 1, 1)
            total = term if total is None else total + term
        out[i] = total


def far_kernel(
    chunks, target, coupling, fetched, out,
    cbuf, fbuf, acc0, acc1, acc2, acc3, csem, fsem,
):
    count, pairs, rank, lanes = coupling.shape
    peers = count // chunks
    rows = peers * pairs * rank

    def fetch(j):
        some = pl.ds(pl.multiple_of(j * peers, peers), peers)
        some_rows = pl.ds(pl.multiple_of(j * rows, rows), rows)
        return (
            pltpu.make_async_copy(fetched.at[some_rows], fbuf.at[some_rows], fsem.at[j]),
            pltpu.make_async_copy(coupling.at[some], cbuf.at[some], csem.at[j]),
        )

    @pl.loop(0, chunks)
    def _(j):
        for copy in fetch(j):
            copy.start()

    evens, odds = (acc0, acc1), (acc2, acc3)
    for acc in evens + odds:
        acc[...] = jnp.zeros_like(acc)
    left = left_lanes((rank, lanes))
    side = lanes // 2

    @pl.loop(0, chunks)
    def _(j):
        for copy in fetch(j):
            copy.wait()
        for i in range(peers):
            p = j * peers + i
            for q in range(pairs):
                v = fbuf[pl.ds(pl.multiple_of((p * pairs + q) * rank, rank), rank), :]
                zero = jnp.zeros_like(v)
                u = jnp.concatenate([jnp.where(left, v, zero), jnp.where(left, zero, v)], axis=0)
                product = contract(cbuf[p, q], u, 1, 0)
                turn = (i * pairs + q) % len(evens)
                evens[turn][target[2 * q, 0, p]] += product
                odds[turn][target[2 * q + 1, 0, p]] += product

    for c in range(out.shape[0]):
        even = sum(acc[c] for acc in evens)
        odd = sum(acc[c] for acc in odds)
        out[c] = jnp.where(left, even, odd)


def edge_kernel(
    bounds, batch, listed, sums, near, basis, transfer, low, high, blocks, out, edge, total, held, sems
):
    leaves, reach = near.shape[0], low.shape[0]
    side = sums.shape[2] // 2
    slots = held.shape[0]
    groups = listed[listed.shape[0] - 1]
    batches = jnp.minimum(slots // batch, (groups * GROUP + batch - 1) // batch)

    def fetch(i, slot):
        entry = listed[i]
        block = blocks.at[(entry >> 16) & 255, (entry >> 8) & 255]
        return pltpu.make_async_copy(block, held.at[slot], sems.at[slot])

    def add(i, slot, count):
        terms = [contract(edge[listed[i + k] & 255], held[slot + k], 1, 1) for k in range(count)]
        for k in range(count):
            total[listed[i + k] >> 24] += terms[k]

    @pl.loop(0, batches * batch)
    def _(i):
        fetch(i, i).start()

    edge[pl.ds(0, reach)] = low[...]
    edge[pl.ds(reach, reach)] = high[...]

    def both_sides(x):
        return (x + pltpu.roll(x, side, 1))[:, :side]

    down = [both_sides(sums[c]) for c in range(sums.shape[0])]
    for depth in range(LEVELS - 2, -1, -1):
        lo, size = bounds[depth]
        above = bounds[depth + 1][0]
        for c in range(size):
            parent = jnp.concatenate(split_pair(down[above + c // 2]), axis=1)
            down[lo + c] = down[lo + c] + both_sides(contract(transfer[lo + c], parent, 1, 0))
    for leaf in range(leaves):
        block = basis[leaf]
        far_leaf = contract(
            jnp.concatenate(split_pair(down[leaf]), axis=0),
            jnp.concatenate([block, block], axis=0),
            0,
            0,
        )
        total[leaf] = near[leaf] + far_leaf

    @pl.loop(0, batches)
    def _(j):
        for k in range(batch):
            fetch(j * batch + k, j * batch + k).wait()
        add(j * batch, j * batch, batch)

    @pl.loop(slots // GROUP, groups)
    def _(g):
        for k in range(GROUP):
            fetch(g * GROUP + k, k).start()
        for k in range(GROUP):
            fetch(g * GROUP + k, k).wait()
        add(g * GROUP, 0, GROUP)

    out[...] = total[pl.ds(0, leaves)].astype(BF16)


def far_call(clusters, target, coupled, fetched, chunks=8):
    peers, pairs, rank, lanes = coupled.shape
    return pl.pallas_call(
        functools.partial(far_kernel, chunks),
        grid_spec=pltpu.PrefetchScalarGridSpec(
            num_scalar_prefetch=1,
            grid=(),
            in_specs=[pl.BlockSpec(memory_space=pl.ANY)] * 2,
            out_specs=pl.BlockSpec(memory_space=pltpu.VMEM),
            scratch_shapes=[
                pltpu.VMEM(coupled.shape, BF16),
                pltpu.VMEM(fetched.shape, BF16),
                *[pltpu.VMEM((clusters + 1, rank, lanes), F32)] * 4,
                pltpu.SemaphoreType.DMA((chunks,)),
                pltpu.SemaphoreType.DMA((chunks,)),
            ],
        ),
        out_shape=jax.ShapeDtypeStruct((clusters, rank, lanes), F32),
        compiler_params=pltpu.CompilerParams(vmem_limit_bytes=48 << 20),
        cost_estimate=pl.CostEstimate(
            flops=4 * fetched.size * rank, bytes_accessed=4 * fetched.size, transcendentals=0
        ),
        name="far",
    )(target, coupled, fetched)


def edge_call(bounds, listed, sums, near, basis, transfer, low, high, blocks, slots=32, batch=8):
    leaves, width, panels = near.shape
    return pl.pallas_call(
        functools.partial(edge_kernel, bounds, batch),
        grid_spec=pltpu.PrefetchScalarGridSpec(
            num_scalar_prefetch=1,
            grid=(),
            in_specs=[pl.BlockSpec(memory_space=pltpu.VMEM)] * 6
            + [pl.BlockSpec(memory_space=pl.ANY)],
            out_specs=pl.BlockSpec(memory_space=pltpu.VMEM),
            scratch_shapes=[
                pltpu.VMEM((2 * low.shape[0], width, panels), BF16),
                pltpu.VMEM((leaves + 1, width, panels), F32),
                pltpu.VMEM((slots, panels, panels), BF16),
                pltpu.SemaphoreType.DMA((slots,)),
            ],
        ),
        out_shape=jax.ShapeDtypeStruct(near.shape, BF16),
        compiler_params=pltpu.CompilerParams(vmem_limit_bytes=48 << 20),
        name="edge",
    )(listed, sums, near, basis, transfer, low, high, blocks)


def whole(shape):
    return pl.BlockSpec(shape, lambda *_: (0,) * len(shape))


def shards(
    charges, leaf_basis, transfer, near_blocks, near_source, coupling, send_cluster, target_cluster
):
    leaves, panels, width = charges.shape
    rank = leaf_basis.shape[2]
    peers, slots = send_cluster.shape[1:]
    near = near_source.shape[1]
    bounds, clusters = level_bounds(leaves)
    pairs = slots // 2
    lanes = 2 * width
    coupled = coupling[0].reshape(peers, pairs, 2, rank, rank)
    coupled = jnp.swapaxes(coupled, 2, 3).reshape(peers, pairs, rank, 2 * rank)
    reach = leaves // 2
    outer, inner = lax.axis_size("gx"), lax.axis_size("gy")
    count = outer * inner

    charges_t = jnp.swapaxes(charges, 1, 2)
    basis_t = jnp.swapaxes(leaf_basis, 1, 2)
    matrices = transfer[0]
    send = jnp.transpose(send_cluster, (2, 0, 1))
    target = jnp.transpose(target_cluster, (2, 0, 1))
    source = jnp.transpose(near_source, (1, 0))

    up = [(i, i + 1) for i in range(count - 1)]
    low = lax.ppermute(charges_t[leaves - reach :], AXES, up)
    high = lax.ppermute(charges_t[:reach], AXES, [(b, a) for a, b in up])

    chunks = 8
    packed = pl.pallas_call(
        functools.partial(up_kernel, bounds, slots),
        grid_spec=pltpu.PrefetchScalarGridSpec(
            num_scalar_prefetch=1,
            grid=(),
            in_specs=[pl.BlockSpec(memory_space=pltpu.VMEM)] * 3,
            out_specs=pl.BlockSpec(memory_space=pl.ANY),
            scratch_shapes=[
                pltpu.VMEM((clusters, rank, lanes), BF16),
                pltpu.VMEM((chunks, peers * pairs * rank // chunks, lanes), BF16),
                pltpu.SemaphoreType.DMA((chunks,)),
            ],
        ),
        out_shape=jax.ShapeDtypeStruct((peers * pairs * rank, lanes), BF16),
        cost_estimate=pl.CostEstimate(
            flops=2 * leaves * panels * rank * width,
            bytes_accessed=2 * peers * slots * rank * width,
            transcendentals=0,
        ),
        name="up_pick",
    )(send, charges_t, basis_t, matrices)

    fetched = lax.all_to_all(packed, AXES, split_axis=0, concat_axis=0, tiled=True)

    per_step = 4
    first = (lax.axis_index(AXES) * leaves).reshape(1)
    near_field, listed = pl.pallas_call(
        functools.partial(near_kernel, reach),
        grid_spec=pltpu.PrefetchScalarGridSpec(
            num_scalar_prefetch=2,
            grid=(leaves // per_step,),
            in_specs=[
                whole((leaves, width, panels)),
                pl.BlockSpec((per_step, near, panels, panels), lambda i, *_: (i, 0, 0, 0)),
            ],
            out_specs=[
                pl.BlockSpec((per_step, width, panels), lambda i, *_: (i, 0, 0)),
                pl.BlockSpec(memory_space=pltpu.SMEM),
            ],
            scratch_shapes=[pltpu.VMEM((leaves + 2 * reach, width, panels), BF16)],
        ),
        out_shape=[
            jax.ShapeDtypeStruct((leaves, width, panels), F32),
            jax.ShapeDtypeStruct((leaves * near + GROUP + 1,), jnp.int32),
        ],
        cost_estimate=pl.CostEstimate(
            flops=2 * leaves * near * panels * panels * width,
            bytes_accessed=2 * leaves * near * panels * panels,
            transcendentals=0,
        ),
        compiler_params=pltpu.CompilerParams(vmem_limit_bytes=24 << 20),
        name="near",
    )(first, source, charges_t, near_blocks)

    sums = far_call(clusters, target, coupled, fetched)
    low, high, sums = lax.optimization_barrier((low, high, sums))
    potential_t = edge_call(
        bounds, listed, sums, near_field, basis_t, matrices, low, high, near_blocks
    )
    return jnp.swapaxes(potential_t, 1, 2)


def solution(mesh):
    placed = (
        P(AXES, None, None),
        P(AXES, None, None),
        P(AXES, None, None, None),
        P(AXES, None, None, None),
        P(AXES, None),
        P(AXES, None, None, None, None),
        P(AXES, None, None),
        P(AXES, None, None),
    )
    return jax.shard_map(
        shards, mesh=mesh, in_specs=placed, out_specs=P(AXES, None, None), check_vma=False
    )
```

profile of v0, /device:TPU:10, one launch (start us, length us, event | category | flops | bytes accessed | tf_op | source)
XLA Modules:
  0.0 105.1 jit_solution(16467665996873533250)
XLA Ops:
  0.0 5.9 %up_pick.1 = bf16[24576,128]{1,0:T(8,128)(2,1)} custom-call(s32[6,1,128]{2,1,0:T(1,128)} %bitcast.26, bf16[16,64,256]{2,1,0:T(8,128)(2,1)} %bitcast.14, bf16[16,64,256]{2,1,0:T(8,128)(2,1)} %bitcast.17, bf16[24,64,64]{2,1,0:T(8,128)(2,1)} %bitcast.19), custom_call_target="tpu_custom_call" | custom-call | flops 33554432 | bytes 6291456 | tf_op jit(solution)/shard_map/up_pick/pallas_call | solution.py:320
  5.9 0.0 copy-start.1
  5.9 10.8 %all-to-all-start = ((bf16[128,192,128]{2,1,0:T(8,128)(2,1)}), bf16[128,192,128]{2,1,0:T(8,128)(2,1)}, u32[]{:S(2)}, u32[]{:S(2)}) async-start(bf16[128,192,128]{2,1,0:T(8,128)(2,1)} %bitcast.23), calls=%async_computation | async-start | bytes 12582912 | tf_op jit(solution)/shard_map/all_to_all | solution.py:342
  16.7 0.0 copy-done.1
  16.8 3.4 %collective-permute-start = (bf16[8,64,256]{2,1,0:T(8,128)(2,1)S(1)}, bf16[8,64,256]{2,1,0:T(8,128)(2,1)S(1)}, u32[]{:S(2)}, u32[]{:S(2)}) collective-permute-start(bf16[8,64,256]{2,1,0:T(8,128)(2,1)S(1)} %get-tuple-element.16), channel_id=1, source_target_pairs={{0,1},{1,2},{2,3},{3,4},{4,5},{5,6},{6,7},{7,8},{8,9},{9,10},{10,1... | collective-permute-start | bytes 786440 | tf_op jit(solution)/shard_map/ppermute | solution.py:316
  20.2 2.5 %collective-permute-start.1 = (bf16[8,64,256]{2,1,0:T(8,128)(2,1)S(1)}, bf16[8,64,256]{2,1,0:T(8,128)(2,1)S(1)}, u32[]{:S(2)}, u32[]{:S(2)}) collective-permute-start(bf16[8,64,256]{2,1,0:T(8,128)(2,1)S(1)} %get-tuple-element.15), channel_id=1, source_target_pairs={{1,0},{2,1},{3,2},{4,3},{5,4},{6,5},{7,6},{8,7},{9,8},{10,9},{11,1... | collective-permute-start | bytes 786440 | tf_op jit(solution)/shard_map/ppermute | solution.py:317
  22.6 7.6 %copy.11 = bf16[128,3,64,2,64]{0,4,3,2,1:T(8,128)(2,1)} copy(bf16[128,3,64,2,64]{0,4,2,3,1:T(8,128)(2,1)} %bitcast.25) | data formatting | bytes 12582912 | tf_op jit(solution)/shard_map/transpose | solution.py:303
  30.2 0.0 copy-start.4
  30.2 9.1 %copy.12.coupling = bf16[128,3,64,128]{3,2,1,0:T(8,128)(2,1)} copy(bf16[128,3,64,128]{0,3,2,1:T(8,128)(2,1)} %bitcast.24) | data formatting | bytes 12582912 | tf_op jit(solution)/shard_map/reshape | solution.py:303
  39.3 0.0 copy-done.4
  39.3 0.0 copy-start
  39.3 4.6 %copy-done = bf16[16,6,256,256]{3,2,1,0:T(8,128)(2,1)S(1)} copy-done((bf16[16,6,256,256]{3,2,1,0:T(8,128)(2,1)S(1)}, bf16[16,6,256,256]{3,2,1,0:T(8,128)(2,1)}, u32[]{:S(2)}) %copy-start) | copy-done | bytes 12582936
  43.9 0.0 copy-start.5
  43.9 5.8 %near.1 = (f32[16,64,256]{2,1,0:T(8,128)S(1)}, s32[101]{0:T(128)S(1)}) custom-call(s32[1]{0:T(128)} %bitcast.first, s32[6,16]{1,0:T(8,128)S(1)} %bitcast.21, bf16[16,64,256]{2,1,0:T(8,128)(2,1)S(1)} %bitcast.16, bf16[16,6,256,256]{3,2,1,0:T(8,128)(2,1)S(1)} %copy-done), custom_call_target="tpu_custom_call" | custom-call | flops 805306368 | bytes 12582912 | tf_op jit(solution)/shard_map/near/pallas_call | solution.py:346
  49.7 43.7 %all-to-all-done = bf16[128,192,128]{2,1,0:T(8,128)(2,1)} async-done(((bf16[128,192,128]{2,1,0:T(8,128)(2,1)}), bf16[128,192,128]{2,1,0:T(8,128)(2,1)}, u32[]{:S(2)}, u32[]{:S(2)}) %all-to-all-start) | async-done | bytes 6291488 | tf_op jit(solution)/shard_map/all_to_all | solution.py:342
  93.4 0.0 copy-done.5
  93.4 0.0 copy-start.2
  93.4 0.0 copy-start.3
  93.4 6.7 %far.1.sums = f32[28,64,128]{2,1,0:T(8,128)S(1)} custom-call(s32[6,1,128]{2,1,0:T(1,128)S(1)} %bitcast.22, bf16[128,3,64,128]{3,2,1,0:T(8,128)(2,1)} %copy.12.coupling, bf16[24576,128]{1,0:T(8,128)(2,1)} %bitcast.11.fetched), custom_call_target="tpu_custom_call" | custom-call | flops 805306368 | bytes 12582912 | tf_op jit(solution)/shard_map/far/pallas_call | solution.py:241
  100.2 0.0 collective-permute-done.low
  100.2 0.0 collective-permute-done.1.high
  100.2 0.0 copy-done.2
  100.2 0.0 copy-done.3
  100.2 4.9 %edge.1 = bf16[16,64,256]{2,1,0:T(8,128)(2,1)} custom-call(s32[101]{0:T(128)S(1)} %get-tuple-element.10.listed, f32[28,64,128]{2,1,0:T(8,128)S(1)} %far.1.sums, f32[16,64,256]{2,1,0:T(8,128)S(1)} %get-tuple-element.12.near, bf16[16,64,256]{2,1,0:T(8,128)(2,1)S(1)} %bitcast.18, bf16[24,64,64]{2,1,0:T(8,128)(2,1)S(1)} %bitcast.20, ...), custom_call_target="tpu_custom_call" | custom-call | tf_op jit(solution)/shard_map/edge/pallas_call | solution.py:267
  (1 shorter events, 0.0 us)
Async XLA Ops:
  5.9 10.8 %copy-start.1 = (bf16[16,256,64]{1,2,0:T(8,128)(2,1)S(1)}, bf16[16,256,64]{1,2,0:T(8,128)(2,1)}, u32[]{:S(2)}) copy-start(bf16[16,256,64]{1,2,0:T(8,128)(2,1)} %param.8) | copy-start | bytes 1572868
  5.9 87.5 %all-to-all-start = ((bf16[128,192,128]{2,1,0:T(8,128)(2,1)}), bf16[128,192,128]{2,1,0:T(8,128)(2,1)}, u32[]{:S(2)}, u32[]{:S(2)}) async-start(bf16[128,192,128]{2,1,0:T(8,128)(2,1)} %bitcast.23), calls=%async_computation | async-start | bytes 12582912 | tf_op jit(solution)/shard_map/all_to_all | solution.py:342
  16.8 83.4 %collective-permute-start = (bf16[8,64,256]{2,1,0:T(8,128)(2,1)S(1)}, bf16[8,64,256]{2,1,0:T(8,128)(2,1)S(1)}, u32[]{:S(2)}, u32[]{:S(2)}) collective-permute-start(bf16[8,64,256]{2,1,0:T(8,128)(2,1)S(1)} %get-tuple-element.16), channel_id=1, source_target_pairs={{0,1},{1,2},{2,3},{3,4},{4,5},{5,6},{6,7},{7,8},{8,9},{9,10},{10,1... | collective-permute-start | bytes 786440 | tf_op jit(solution)/shard_map/ppermute | solution.py:316
  20.2 80.0 %collective-permute-start.1 = (bf16[8,64,256]{2,1,0:T(8,128)(2,1)S(1)}, bf16[8,64,256]{2,1,0:T(8,128)(2,1)S(1)}, u32[]{:S(2)}, u32[]{:S(2)}) collective-permute-start(bf16[8,64,256]{2,1,0:T(8,128)(2,1)S(1)} %get-tuple-element.15), channel_id=1, source_target_pairs={{1,0},{2,1},{3,2},{4,3},{5,4},{6,5},{7,6},{8,7},{9,8},{10,9},{11,1... | collective-permute-start | bytes 786440 | tf_op jit(solution)/shard_map/ppermute | solution.py:317
  30.2 9.1 %copy-start.4 = (s32[16,6]{0,1:T(8,128)S(1)}, s32[16,6]{0,1:T(8,128)}, u32[]{:S(2)}) copy-start(s32[16,6]{0,1:T(8,128)} %param.12) | copy-start | bytes 1156
  39.3 4.6 %copy-start = (bf16[16,6,256,256]{3,2,1,0:T(8,128)(2,1)S(1)}, bf16[16,6,256,256]{3,2,1,0:T(8,128)(2,1)}, u32[]{:S(2)}) copy-start(bf16[16,6,256,256]{3,2,1,0:T(8,128)(2,1)} %blocks.3) | copy-start | bytes 37748740
  43.9 49.6 %copy-start.5 = (s32[1,128,6]{1,0,2:T(1,128)S(1)}, s32[1,128,6]{1,0,2:T(1,128)}, u32[]{:S(2)}) copy-start(s32[1,128,6]{1,0,2:T(1,128)} %param.15) | copy-start | bytes 9220
  93.4 6.8 %copy-start.2 = (bf16[16,256,64]{1,2,0:T(8,128)(2,1)S(1)}, bf16[16,256,64]{1,2,0:T(8,128)(2,1)}, u32[]{:S(2)}) copy-start(bf16[16,256,64]{1,2,0:T(8,128)(2,1)} %param.9) | copy-start | bytes 1572868
  93.4 6.8 %copy-start.3 = (bf16[1,24,64,64]{3,2,1,0:T(8,128)(2,1)S(1)}, bf16[1,24,64,64]{3,2,1,0:T(8,128)(2,1)}, u32[]{:S(2)}) copy-start(bf16[1,24,64,64]{3,2,1,0:T(8,128)(2,1)} %param.10) | copy-start | bytes 589828
where the time goes:
time: 105 us
  waiting for transfers between devices  43.7 us (42%)
  Pallas kernels  23.3 us (22%)
  local copies, waits for them, and re-layouts  21.3 us (20%)
  starting transfers between devices  16.7 us (16%)
    all_to_all x1, waiting for transfers between devices, shards(): lax.all_to_all(packed, AXES, split_axis=0, concat_axis=0, tiled=True)  43.7 us
    all_to_all x1, starting transfers between devices, shards(): lax.all_to_all(packed, AXES, split_axis=0, concat_axis=0, tiled=True)  10.8 us
    reshape x1, local copies, waits for them, and re-layouts, shards(): coupled = jnp.swapaxes(coupled, 2, 3).reshape(peers, pairs, rank, 2 * rank)  9.07 us
    transpose x1, local copies, waits for them, and re-layouts, shards(): coupled = jnp.swapaxes(coupled, 2, 3).reshape(peers, pairs, rank, 2 * rank)  7.59 us
    pallas_call x1, Pallas kernels, far_call(): pl.pallas_call(functools.partial(far_kernel, chunks), grid_spec=pltpu.Pre...  6.72 us
    pallas_call x1, Pallas kernels, shards(): pl.pallas_call(functools.partial(up_kernel, bounds, slots), grid_spec=plt...  5.87 us
    pallas_call x1, Pallas kernels, shards(): pl.pallas_call(functools.partial(near_kernel, reach), grid_spec=pltpu.Pre...  5.83 us
    pallas_call x1, Pallas kernels, edge_call(): pl.pallas_call(functools.partial(edge_kernel, bounds, batch), grid_spec=p...  4.92 us
  transfers between devices with their start and end apart: 3, of which 1 were waited for; matrix products, arithmetic and copies ran while one was open for 16% of the time, Pallas kernels for 12%

commit v1 on v0

--- a/solution.py
+++ b/solution.py
@@ -75,7 +75,7 @@
                 staged[j, pl.ds(at, rank), :] = jnp.where(left, even, odd)
             return carry
 
-        lax.fori_loop(0, per_chunk, copy, 0, unroll=16)
+        lax.fori_loop(0, per_chunk, copy, 0, unroll=8)
         send_out(j).start()
 
     @pl.loop(0, chunks)
@@ -236,7 +236,7 @@
     out[...] = total[pl.ds(0, leaves)].astype(BF16)
 
 
-def far_call(clusters, target, coupled, fetched, chunks=8):
+def far_call(clusters, target, coupled, fetched, chunks=4):
     peers, pairs, rank, lanes = coupled.shape
     return pl.pallas_call(
         functools.partial(far_kernel, chunks),
@@ -316,7 +316,7 @@
     low = lax.ppermute(charges_t[leaves - reach :], AXES, up)
     high = lax.ppermute(charges_t[:reach], AXES, [(b, a) for a, b in up])
 
-    chunks = 8
+    chunks = 16
     packed = pl.pallas_call(
         functools.partial(up_kernel, bounds, slots),
         grid_spec=pltpu.PrefetchScalarGridSpec(
@@ -341,7 +341,7 @@
 
     fetched = lax.all_to_all(packed, AXES, split_axis=0, concat_axis=0, tiled=True)
 
-    per_step = 4
+    per_step = 8
     first = (lax.axis_index(AXES) * leaves).reshape(1)
     near_field, listed = pl.pallas_call(
         functools.partial(near_kernel, reach),

time: 105 us -> 105 us (level)
  no operation moved by 1% of the time
where the time goes in v1:
time: 105 us; the launch traced here: 104 us
  waiting for transfers between devices  44 us (42%)
  Pallas kernels  22.3 us (21%)
  local copies, waits for them, and re-layouts  21.3 us (20%)
  starting transfers between devices  16.7 us (16%)
    all_to_all x1, waiting for transfers between devices, shards(): lax.all_to_all(packed, AXES, split_axis=0, concat_axis=0, tiled=True)  44 us
    all_to_all x1, starting transfers between devices, shards(): lax.all_to_all(packed, AXES, split_axis=0, concat_axis=0, tiled=True)  10.8 us
    reshape x1, local copies, waits for them, and re-layouts, shards(): coupled = jnp.swapaxes(coupled, 2, 3).reshape(peers, pairs, rank, 2 * rank)  9.07 us
    transpose x1, local copies, waits for them, and re-layouts, shards(): coupled = jnp.swapaxes(coupled, 2, 3).reshape(peers, pairs, rank, 2 * rank)  7.59 us
    pallas_call x1, Pallas kernels, far_call(): pl.pallas_call(functools.partial(far_kernel, chunks), grid_spec=pltpu.Pre...  6.58 us
    pallas_call x1, Pallas kernels, shards(): pl.pallas_call(functools.partial(up_kernel, bounds, slots), grid_spec=plt...  5.82 us
    pallas_call x1, Pallas kernels, shards(): pl.pallas_call(functools.partial(near_kernel, reach), grid_spec=pltpu.Pre...  5.53 us
    unnamed x12, local copies, waits for them, and re-layouts  4.6 us
  transfers between devices with their start and end apart: 3, of which 1 were waited for; matrix products, arithmetic and copies ran while one was open for 16% of the time, Pallas kernels for 12%

profile of v1, /device:TPU:10, one launch (start us, length us, event | category | flops | bytes accessed | tf_op | source)
XLA Modules:
  0.0 104.4 jit_solution(695027175578178755)
XLA Ops:
  0.0 5.8 %up_pick.1 = bf16[24576,128]{1,0:T(8,128)(2,1)} custom-call(s32[6,1,128]{2,1,0:T(1,128)} %bitcast.26, bf16[16,64,256]{2,1,0:T(8,128)(2,1)} %bitcast.14, bf16[16,64,256]{2,1,0:T(8,128)(2,1)} %bitcast.17, bf16[24,64,64]{2,1,0:T(8,128)(2,1)} %bitcast.19), custom_call_target="tpu_custom_call" | custom-call | flops 33554432 | bytes 6291456 | tf_op jit(solution)/shard_map/up_pick/pallas_call | solution.py:320
  5.8 0.0 copy-start.1
  5.8 10.8 %all-to-all-start = ((bf16[128,192,128]{2,1,0:T(8,128)(2,1)}), bf16[128,192,128]{2,1,0:T(8,128)(2,1)}, u32[]{:S(2)}, u32[]{:S(2)}) async-start(bf16[128,192,128]{2,1,0:T(8,128)(2,1)} %bitcast.23), calls=%async_computation | async-start | bytes 12582912 | tf_op jit(solution)/shard_map/all_to_all | solution.py:342
  16.7 0.0 copy-done.1
  16.7 3.4 %collective-permute-start = (bf16[8,64,256]{2,1,0:T(8,128)(2,1)S(1)}, bf16[8,64,256]{2,1,0:T(8,128)(2,1)S(1)}, u32[]{:S(2)}, u32[]{:S(2)}) collective-permute-start(bf16[8,64,256]{2,1,0:T(8,128)(2,1)S(1)} %get-tuple-element.16), channel_id=1, source_target_pairs={{0,1},{1,2},{2,3},{3,4},{4,5},{5,6},{6,7},{7,8},{8,9},{9,10},{10,1... | collective-permute-start | bytes 786440 | tf_op jit(solution)/shard_map/ppermute | solution.py:316
  20.1 2.5 %collective-permute-start.1 = (bf16[8,64,256]{2,1,0:T(8,128)(2,1)S(1)}, bf16[8,64,256]{2,1,0:T(8,128)(2,1)S(1)}, u32[]{:S(2)}, u32[]{:S(2)}) collective-permute-start(bf16[8,64,256]{2,1,0:T(8,128)(2,1)S(1)} %get-tuple-element.15), channel_id=1, source_target_pairs={{1,0},{2,1},{3,2},{4,3},{5,4},{6,5},{7,6},{8,7},{9,8},{10,9},{11,1... | collective-permute-start | bytes 786440 | tf_op jit(solution)/shard_map/ppermute | solution.py:317
  22.6 7.6 %copy.11 = bf16[128,3,64,2,64]{0,4,3,2,1:T(8,128)(2,1)} copy(bf16[128,3,64,2,64]{0,4,2,3,1:T(8,128)(2,1)} %bitcast.25) | data formatting | bytes 12582912 | tf_op jit(solution)/shard_map/transpose | solution.py:303
  30.2 0.0 copy-start.4
  30.2 9.1 %copy.12.coupling = bf16[128,3,64,128]{3,2,1,0:T(8,128)(2,1)} copy(bf16[128,3,64,128]{0,3,2,1:T(8,128)(2,1)} %bitcast.24) | data formatting | bytes 12582912 | tf_op jit(solution)/shard_map/reshape | solution.py:303
  39.3 0.0 copy-done.4
  39.3 0.0 copy-start
  39.3 4.6 %copy-done = bf16[16,6,256,256]{3,2,1,0:T(8,128)(2,1)S(1)} copy-done((bf16[16,6,256,256]{3,2,1,0:T(8,128)(2,1)S(1)}, bf16[16,6,256,256]{3,2,1,0:T(8,128)(2,1)}, u32[]{:S(2)}) %copy-start) | copy-done | bytes 12582936
  43.8 0.0 copy-start.5
  43.8 5.5 %near.1 = (f32[16,64,256]{2,1,0:T(8,128)S(1)}, s32[101]{0:T(128)S(1)}) custom-call(s32[1]{0:T(128)} %bitcast.first, s32[6,16]{1,0:T(8,128)S(1)} %bitcast.21, bf16[16,64,256]{2,1,0:T(8,128)(2,1)S(1)} %bitcast.16, bf16[16,6,256,256]{3,2,1,0:T(8,128)(2,1)S(1)} %copy-done), custom_call_target="tpu_custom_call" | custom-call | flops 805306368 | bytes 12582912 | tf_op jit(solution)/shard_map/near/pallas_call | solution.py:346
  49.4 44.0 %all-to-all-done = bf16[128,192,128]{2,1,0:T(8,128)(2,1)} async-done(((bf16[128,192,128]{2,1,0:T(8,128)(2,1)}), bf16[128,192,128]{2,1,0:T(8,128)(2,1)}, u32[]{:S(2)}, u32[]{:S(2)}) %all-to-all-start) | async-done | bytes 6291488 | tf_op jit(solution)/shard_map/all_to_all | solution.py:342
  93.4 0.0 copy-done.5
  93.4 0.0 copy-start.2
  93.4 0.0 copy-start.3
  93.4 6.6 %far.1.sums = f32[28,64,128]{2,1,0:T(8,128)S(1)} custom-call(s32[6,1,128]{2,1,0:T(1,128)S(1)} %bitcast.22, bf16[128,3,64,128]{3,2,1,0:T(8,128)(2,1)} %copy.12.coupling, bf16[24576,128]{1,0:T(8,128)(2,1)} %bitcast.11.fetched), custom_call_target="tpu_custom_call" | custom-call | flops 805306368 | bytes 12582912 | tf_op jit(solution)/shard_map/far/pallas_call | solution.py:241
  100.0 0.0 collective-permute-done.low
  100.0 0.0 collective-permute-done.1.high
  100.0 0.0 copy-done.2
  100.0 0.0 copy-done.3
  100.0 4.4 %edge.1 = bf16[16,64,256]{2,1,0:T(8,128)(2,1)} custom-call(s32[101]{0:T(128)S(1)} %get-tuple-element.10.listed, f32[28,64,128]{2,1,0:T(8,128)S(1)} %far.1.sums, f32[16,64,256]{2,1,0:T(8,128)S(1)} %get-tuple-element.12.near, bf16[16,64,256]{2,1,0:T(8,128)(2,1)S(1)} %bitcast.18, bf16[24,64,64]{2,1,0:T(8,128)(2,1)S(1)} %bitcast.20, ...), custom_call_target="tpu_custom_call" | custom-call | tf_op jit(solution)/shard_map/edge/pallas_call | solution.py:267
  (1 shorter events, 0.0 us)
Async XLA Ops:
  5.8 10.8 %copy-start.1 = (bf16[16,256,64]{1,2,0:T(8,128)(2,1)S(1)}, bf16[16,256,64]{1,2,0:T(8,128)(2,1)}, u32[]{:S(2)}) copy-start(bf16[16,256,64]{1,2,0:T(8,128)(2,1)} %param.8) | copy-start | bytes 1572868
  5.8 87.5 %all-to-all-start = ((bf16[128,192,128]{2,1,0:T(8,128)(2,1)}), bf16[128,192,128]{2,1,0:T(8,128)(2,1)}, u32[]{:S(2)}, u32[]{:S(2)}) async-start(bf16[128,192,128]{2,1,0:T(8,128)(2,1)} %bitcast.23), calls=%async_computation | async-start | bytes 12582912 | tf_op jit(solution)/shard_map/all_to_all | solution.py:342
  16.7 83.3 %collective-permute-start = (bf16[8,64,256]{2,1,0:T(8,128)(2,1)S(1)}, bf16[8,64,256]{2,1,0:T(8,128)(2,1)S(1)}, u32[]{:S(2)}, u32[]{:S(2)}) collective-permute-start(bf16[8,64,256]{2,1,0:T(8,128)(2,1)S(1)} %get-tuple-element.16), channel_id=1, source_target_pairs={{0,1},{1,2},{2,3},{3,4},{4,5},{5,6},{6,7},{7,8},{8,9},{9,10},{10,1... | collective-permute-start | bytes 786440 | tf_op jit(solution)/shard_map/ppermute | solution.py:316
  20.1 79.9 %collective-permute-start.1 = (bf16[8,64,256]{2,1,0:T(8,128)(2,1)S(1)}, bf16[8,64,256]{2,1,0:T(8,128)(2,1)S(1)}, u32[]{:S(2)}, u32[]{:S(2)}) collective-permute-start(bf16[8,64,256]{2,1,0:T(8,128)(2,1)S(1)} %get-tuple-element.15), channel_id=1, source_target_pairs={{1,0},{2,1},{3,2},{4,3},{5,4},{6,5},{7,6},{8,7},{9,8},{10,9},{11,1... | collective-permute-start | bytes 786440 | tf_op jit(solution)/shard_map/ppermute | solution.py:317
  30.2 9.1 %copy-start.4 = (s32[16,6]{0,1:T(8,128)S(1)}, s32[16,6]{0,1:T(8,128)}, u32[]{:S(2)}) copy-start(s32[16,6]{0,1:T(8,128)} %param.12) | copy-start | bytes 1156
  39.3 4.6 %copy-start = (bf16[16,6,256,256]{3,2,1,0:T(8,128)(2,1)S(1)}, bf16[16,6,256,256]{3,2,1,0:T(8,128)(2,1)}, u32[]{:S(2)}) copy-start(bf16[16,6,256,256]{3,2,1,0:T(8,128)(2,1)} %blocks.3) | copy-start | bytes 37748740
  43.8 49.6 %copy-start.5 = (s32[1,128,6]{1,0,2:T(1,128)S(1)}, s32[1,128,6]{1,0,2:T(1,128)}, u32[]{:S(2)}) copy-start(s32[1,128,6]{1,0,2:T(1,128)} %param.15) | copy-start | bytes 9220
  93.4 6.6 %copy-start.2 = (bf16[16,256,64]{1,2,0:T(8,128)(2,1)S(1)}, bf16[16,256,64]{1,2,0:T(8,128)(2,1)}, u32[]{:S(2)}) copy-start(bf16[16,256,64]{1,2,0:T(8,128)(2,1)} %param.9) | copy-start | bytes 1572868
  93.4 6.6 %copy-start.3 = (bf16[1,24,64,64]{3,2,1,0:T(8,128)(2,1)S(1)}, bf16[1,24,64,64]{3,2,1,0:T(8,128)(2,1)}, u32[]{:S(2)}) copy-start(bf16[1,24,64,64]{3,2,1,0:T(8,128)(2,1)} %param.10) | copy-start | bytes 589828
